TPU v7x, 128 devices: a whole 4x4x4 slice. The times are simulated.
128 devices in a mesh: row: 8 (over x, core), col: 16 (over y, z).
Axes of the slice: x: 4, y: 4, z: 4, core: 2. Of those that a mesh axis runs over, the one named last changes fastest.
Arguments:
- imu: bfloat16 [32768, 128], P(('row', 'col')), may hold values from -30 to 30
- camera: bfloat16 [16, 2048, 128], P('col', 'row'), may hold values from -30 to 30
- imu_mass: float32 [32768], P('row'), may hold values from 0.3 to 3
- cam_mass: float32 [32768], P('col'), may hold values from 0.3 to 3
Outputs:
- grad_imu: float32 [32768, 128], P(('row', 'col'))
- grad_camera: float32 [16, 2048, 128], P('col', 'row')
All inputs are finite; a program needn't handle non-finite values.
Results may differ from a plain program's by a relative error of at most 0.0028.
Values may be sent and summed in bfloat16 or wider, within the bound.
A program may use at most 128 MiB of HBM per device.

v0:
```python
import math
import jax
import jax.numpy as jnp
from jax import lax
from jax.sharding import PartitionSpec as P

D = 128
ITERS = 3


def cost_block(rows, rows_sq, cols, cols_sq):
    cross = jnp.dot(rows, cols.T, preferred_element_type=jnp.float32)
    return rows_sq[:, None] + cols_sq[None, :] - 2.0 * cross


def squares(values):
    return jnp.sum(jnp.square(values.astype(jnp.float32)), axis=1)


def combine(part, axis):
    parts = lax.all_gather(part, axis, axis=0)
    top = jnp.max(parts, axis=0)
    return top + jnp.log(jnp.sum(jnp.exp(parts - top[None, :]), axis=0))


def local(imu, camera, imu_mass, cam_mass):
    epsilon = D / 20.0
    imu_rows = lax.all_gather(imu, "col", axis=0, tiled=True)
    cam_rows = lax.all_gather(camera, "row", axis=1, tiled=True)[0]
    rows = imu_rows.shape[0]
    cols = cam_rows.shape[0]
    block = math.gcd(rows, 512)
    count = rows // block
    rows_sq = squares(imu_rows)
    cols_sq = squares(cam_rows)
    log_a = jnp.log(imu_mass)
    log_b = jnp.log(cam_mass)
    stored = cost_block(imu_rows, rows_sq, cam_rows, cols_sq)

    def tile(k):
        return lax.dynamic_slice_in_dim(stored, k * block, block, 0)

    blocks = jnp.arange(count, dtype=jnp.int32)

    def row_lse(g):

        def single(k):
            scores = (g[None, :] - tile(k)) / epsilon
            peak = jnp.max(scores, axis=1)
            return (peak, jnp.sum(jnp.exp(scores - peak[:, None]), axis=1))

        peak, total = lax.map(single, blocks)
        peak = peak.reshape(rows)
        total = total.reshape(rows)
        return combine(peak + jnp.log(total), "col")

    def col_lse(f):

        def advance(k, carry):
            peak, total = carry
            f_blk = lax.dynamic_slice_in_dim(f, k * block, block, 0)
            scores = (f_blk[:, None] - tile(k)) / epsilon
            new_peak = jnp.maximum(peak, jnp.max(scores, axis=0))
            total = total * jnp.exp(peak - new_peak) + jnp.sum(
                jnp.exp(scores - new_peak[None, :]), axis=0
            )
            return (new_peak, total)

        start = (jnp.full((cols,), -1e30, jnp.float32), jnp.zeros((cols,), jnp.float32))
        peak, total = lax.fori_loop(0, count, advance, start)
        return combine(peak + jnp.log(total), "row")

    g = jnp.zeros((cols,), jnp.float32)
    f = jnp.zeros((rows,), jnp.float32)
    for step in range(ITERS):
        f = epsilon * log_a - epsilon * row_lse(g)
        g = epsilon * log_b - epsilon * col_lse(f)

    def plan_rows(k):
        f_blk = lax.dynamic_slice_in_dim(f, k * block, block, 0)
        return jnp.exp((f_blk[:, None] + g[None, :] - tile(k)) / epsilon).astype(jnp.bfloat16)

    plan = lax.map(plan_rows, blocks).reshape(rows, cols)
    row_total = jnp.sum(plan, axis=1, dtype=jnp.float32)
    col_total = jnp.sum(plan, axis=0, dtype=jnp.float32)
    imu_share = rows // lax.axis_size("col")
    cam_share = cols // lax.axis_size("row")
    plan_part = plan
    own = imu_rows.astype(jnp.float32)
    weight = row_total
    pulled = jnp.dot(plan_part, cam_rows, preferred_element_type=jnp.float32)
    grad_imu = lax.psum_scatter(
        2.0 * (weight[:, None] * own - pulled), "col", scatter_dimension=0, tiled=True
    )
    plan_part = plan
    own = cam_rows.astype(jnp.float32)
    weight = col_total
    pulled = lax.dot_general(
        plan_part, imu_rows, (((0,), (0,)), ((), ())), preferred_element_type=jnp.float32
    )
    grad_cam = lax.psum_scatter(
        2.0 * (weight[:, None] * own - pulled), "row", scatter_dimension=0, tiled=True
    )
    return (grad_imu, grad_cam[None])


def solution(mesh):
    in_specs = (P(("row", "col"), None), P("col", "row", None), P("row"), P("col"))
    out_specs = (P(("row", "col"), None), P("col", "row", None))
    return jax.shard_map(local, mesh=mesh, in_specs=in_specs, out_specs=out_specs, check_vma=False)
```

profile of v0, /device:TPU:0, one launch (start us, length us, event | category | flops | bytes accessed | tf_op | source)
XLA Modules:
  0.0 668.9 jit_solution(3283846206429722116)
XLA Ops:
  8.0 13.8 %all_gather.37 = bf16[1,2048,128]{2,1,0:T(8,128)(2,1)S(1)} all-gather(bf16[1,256,128]{2,1,0:T(8,128)(2,1)} %param.19), channel_id=1, replica_groups=mesh['row'=8,'col'=16] {'row'}, dimensions={1}, use_global_device_ids=true | all-gather | bytes 589824 | tf_op jit(solution)/shard_map/all_gather | solution.py:29
  22.1 33.4 %all-gather.8.cloned.1.call-done = bf16[4096,128]{1,0:T(8,128)(2,1)} async-done(((bf16[256,128]{1,0:T(8,128)(2,1)}), bf16[4096,128]{1,0:T(8,128)(2,1)}) %all-gather.8.cloned.1.call-update) | async-done | bytes 1048592 | tf_op jit(solution)/shard_map/all_gather | solution.py:28
  57.4 14.3 %multiply_subtract_fusion = f32[4096,2048]{1,0:T(8,128)} fusion(f32[2048]{0:T(1024)S(1)} %fusion.14, f32[4096]{0:T(1024)S(1)} %fusion.13, bf16[4096,128]{1,0:T(8,128)(2,1)} %all-gather.8.cloned.1.call-done, bf16[1,2048,128]{2,1,0:T(8,128)(2,1)S(1)} %all_gather.37), kind=kOutput, calls=%fused_computation.32 | convolution fusion | flops 2172649472 | bytes 35151872 | tf_op jit(solution)/shard_map/dot_general | solution.py:12
  71.7 56.4 %while.94 = (s32[]{:T(128)}, f32[8,512]{1,0:T(8,128)S(1)}, f32[8,512]{1,0:T(8,128)S(1)}, s32[8]{0:T(128)S(1)}, f32[4096,2048]{1,0:T(8,128)}, /*index=5*/s32[]{:T(128)}, s32[1]{0:T(128)}, s32[]{:T(128)}, s32[]{:T(128)}) while((s32[]{:T(128)}, f32[8,512]{1,0:T(8,128)S(1)}, f32[8,512]{1,0:T(8,128)S(1)}, s32[8]{0:T(128)S(1)}, ...), condition=%wide.region_5.6_spmd, body=%wide.region_2.5_spmd.sunk | while | flops 7339014 | bytes 8403111 | solution.py:52
  128.2 23.1 %all-gather.3 = f32[16,1,4096]{2,1,0:T(1,128)S(1)} all-gather(f32[1,1,4096]{2,1,0:T(1,128)S(1)} %reshape.116), channel_id=1, replica_groups=mesh['row'=8,'col'=16] {'col'}, dimensions={0}, use_global_device_ids=true | all-gather | bytes 278528 | tf_op jit(solution)/shard_map/all_gather | solution.py:21
  151.7 47.5 %while.98 = (s32[]{:T(128)}, f32[2048]{0:T(1024)S(1)}, f32[2048]{0:T(1024)S(1)}, f32[4096]{0:T(1024)S(1)}, f32[4096,2048]{1,0:T(8,128)}, /*index=5*/s32[]{:T(128)}, s32[]{:T(128)}, s32[]{:T(128)}, s32[]{:T(128)}) while((s32[]{:T(128)}, f32[2048]{0:T(1024)S(1)}, f32[2048]{0:T(1024)S(1)}, f32[4096]{0:T(1024)S(1)}, ...), condition=%wide.region_11.12_spmd.clone, body=%wide.region_8.11_spmd.clone.sunk | while | flops 7350279 | bytes 8503458 | solution.py:70
  199.2 13.1 %all-gather = f32[16384]{0:T(1024)S(1)} all-gather(f32[2048]{0:T(1024)S(1)} %log_add_fusion.5), channel_id=2, replica_groups=mesh['row'=8,'col'=16] {'row'}, dimensions={0}, use_global_device_ids=true | all-gather | bytes 73728 | tf_op jit(solution)/shard_map/all_gather | solution.py:21
  212.4 57.6 %while.95 = (s32[]{:T(128)}, f32[8,512]{1,0:T(8,128)S(1)}, f32[8,512]{1,0:T(8,128)S(1)}, f32[2048]{0:T(1024)S(1)}, s32[8]{0:T(128)S(1)}, /*index=5*/f32[4096,204...) while((s32[]{:T(128)}, f32[8,512]{1,0:T(8,128)S(1)}, f32[8,512]{1,0:T(8,128)S(1)}, ...), condition=%wide.region_17.18_spmd, body=%wide.region_14.17_spmd.sunk | while | flops 7339014 | bytes 8419503 | solution.py:52
  270.0 21.7 %all-gather.4 = f32[16,1,4096]{2,1,0:T(1,128)S(1)} all-gather(f32[1,1,4096]{2,1,0:T(1,128)S(1)} %reshape.118), channel_id=1, replica_groups=mesh['row'=8,'col'=16] {'col'}, dimensions={0}, use_global_device_ids=true | all-gather | bytes 278528 | tf_op jit(solution)/shard_map/all_gather | solution.py:21
  292.2 47.5 %while.99 = (s32[]{:T(128)}, f32[2048]{0:T(1024)S(1)}, f32[2048]{0:T(1024)S(1)}, f32[4096]{0:T(1024)S(1)}, f32[4096,2048]{1,0:T(8,128)}, /*index=5*/s32[]{:T(128)}, s32[]{:T(128)}, s32[]{:T(128)}, s32[]{:T(128)}) while((s32[]{:T(128)}, f32[2048]{0:T(1024)S(1)}, f32[2048]{0:T(1024)S(1)}, f32[4096]{0:T(1024)S(1)}, ...), condition=%wide.region_23.24_spmd.clone, body=%wide.region_20.23_spmd.clone.sunk | while | flops 7350279 | bytes 8503458 | solution.py:70
  339.7 12.8 %all-gather.1 = f32[16384]{0:T(1024)S(1)} all-gather(f32[2048]{0:T(1024)S(1)} %log_add_fusion.4), channel_id=3, replica_groups=mesh['row'=8,'col'=16] {'row'}, dimensions={0}, use_global_device_ids=true | all-gather | bytes 73728 | tf_op jit(solution)/shard_map/all_gather | solution.py:21
  352.6 56.7 %while.96 = (s32[]{:T(128)}, f32[8,512]{1,0:T(8,128)S(1)}, f32[8,512]{1,0:T(8,128)S(1)}, f32[2048]{0:T(1024)S(1)}, s32[8]{0:T(128)S(1)}, /*index=5*/f32[4096,204...) while((s32[]{:T(128)}, f32[8,512]{1,0:T(8,128)S(1)}, f32[8,512]{1,0:T(8,128)S(1)}, ...), condition=%wide.region_29.30_spmd, body=%wide.region_26.29_spmd.sunk | while | flops 7339014 | bytes 8419503 | solution.py:52
  409.3 23.1 %all-gather.5 = f32[16,1,4096]{2,1,0:T(1,128)S(1)} all-gather(f32[1,1,4096]{2,1,0:T(1,128)S(1)} %reshape.120), channel_id=1, replica_groups=mesh['row'=8,'col'=16] {'col'}, dimensions={0}, use_global_device_ids=true | all-gather | bytes 278528 | tf_op jit(solution)/shard_map/all_gather | solution.py:21
  432.8 47.5 %while.100 = (s32[]{:T(128)}, f32[2048]{0:T(1024)S(1)}, f32[2048]{0:T(1024)S(1)}, f32[4096]{0:T(1024)S(1)}, f32[4096,2048]{1,0:T(8,128)}, /*index=5*/s32[]{:T(128)}, s32[]{:T(128)}, s32[]{:T(128)}, s32[]{:T(128)}) while((s32[]{:T(128)}, f32[2048]{0:T(1024)S(1)}, f32[2048]{0:T(1024)S(1)}, f32[4096]{0:T(1024)S(1)}, ...), condition=%wide.region_35.36_spmd.clone, body=%wide.region_32.35_spmd.clone.sunk | while | flops 7350279 | bytes 8503458 | solution.py:70
  480.3 13.0 %all-gather.2 = f32[16384]{0:T(1024)S(1)} all-gather(f32[2048]{0:T(1024)S(1)} %log_add_fusion.3), channel_id=4, replica_groups=mesh['row'=8,'col'=16] {'row'}, dimensions={0}, use_global_device_ids=true | all-gather | bytes 73728 | tf_op jit(solution)/shard_map/all_gather | solution.py:21
  493.4 45.2 %while.97 = (s32[]{:T(128)}, bf16[8,512,2048]{2,1,0:T(8,128)(2,1)}, s32[8]{0:T(128)S(1)}, f32[4096]{0:T(1024)S(1)}, f32[2048]{0:T(1024)S(1)}, /*index=5*/f32[409...) while((s32[]{:T(128)}, bf16[8,512,2048]{2,1,0:T(8,128)(2,1)}, s32[8]{0:T(128)S(1)}, ...), condition=%wide.region_39.40_spmd, body=%wide.region_38.39_spmd.sunk | while | flops 4194310 | bytes 6306471 | solution.py:83
  500.3 4.4 fusion.40
  517.3 4.4 fusion.40
  528.5 4.4 fusion.40
  538.5 8.5 %convert_reduce_fusion = (f32[2048]{0:T(1024)S(1)}, f32[8,512]{1,0:T(8,128)S(1)}) fusion(bf16[8,512,2048]{2,1,0:T(8,128)(2,1)} %get-tuple-element.425), kind=kLoop, calls=%fused_computation.30 | loop fusion | flops 25159680 | bytes 16801792 | tf_op jit(solution)/shard_map/reduce_sum | solution.py:85
  549.2 6.0 fusion.12
  555.3 11.7 %fusion.11 = f32[4096,128]{1,0:T(8,128)} fusion(bf16[4096,2048]{1,0:T(8,128)(2,1)} %bitcast.69, bf16[4096,128]{1,0:T(8,128)(2,1)S(1)} %copy-done.1, f32[4096]{0:T(1024)S(1)} %bitcast.78, bf16[1,2048,128]{2,1,0:T(8,128)(2,1)S(1)} %all_gather.37), kind=kOutput, calls=%fused_computation.34 | convolution fusion | flops 2149580800 | bytes 20463616 | tf_op jit(solution)/shard_map/dot_general | solution.py:91
  567.0 18.1 %reduce-scatter.5.cloned.1.call-done = f32[256,128]{1,0:T(8,128)} async-done(((f32[2048,128]{1,0:T(8,128)}), f32[256,128]{1,0:T(8,128)}) %reduce-scatter.5.cloned.1.call-update) | async-done | bytes 131088 | tf_op jit(solution)/shard_map/reduce_scatter | solution.py:101
  585.1 77.2 %reduce-scatter.3.cloned.1.call-done = f32[256,128]{1,0:T(8,128)} async-done(((f32[4096,128]{1,0:T(8,128)}), f32[256,128]{1,0:T(8,128)}) %reduce-scatter.3.cloned.1.call-update) | async-done | bytes 131088 | tf_op jit(solution)/shard_map/reduce_scatter | solution.py:92
  (349 shorter events, 330.3 us)
Async XLA Ops:
  7.2 48.4 %all-gather.8.cloned.1.call-start = ((), (), s32[]{:S(2)}) async-start(), calls=%async_computation.2 | async-start | bytes 1114112 | tf_op jit(solution)/shard_map/all_gather | solution.py:28
  7.9 577.2 %reduce-scatter.5.cloned.1.call-start = ((), (), s32[]{:S(2)}) async-start(), calls=%async_computation.4 | async-start | bytes 1179648 | tf_op jit(solution)/shard_map/reduce_scatter | solution.py:101
  71.7 80.0 %copy-start.2 = (f32[4096]{0:T(1024)S(1)}, f32[4096]{0:T(1024)}, u32[]{:S(2)}) copy-start(f32[4096]{0:T(1024)} %param.20) | copy-start | bytes 49156
  151.7 60.7 %copy-start.3 = (f32[2048]{0:T(1024)S(1)}, f32[2048]{0:T(1024)}, u32[]{:S(2)}) copy-start(f32[2048]{0:T(1024)} %param.21) | copy-start | bytes 24580
  493.3 53.7 %copy-start.1 = (bf16[4096,128]{1,0:T(8,128)(2,1)S(1)}, bf16[4096,128]{1,0:T(8,128)(2,1)}, u32[]{:S(2)}) copy-start(bf16[4096,128]{1,0:T(8,128)(2,1)} %all-gather.8.cloned.1.call-done) | copy-start | bytes 3145732
  538.5 10.7 %copy-start = (bf16[8,512,2048]{2,1,0:T(8,128)(2,1)S(1)}, bf16[8,512,2048]{2,1,0:T(8,128)(2,1)}, u32[]{:S(2)}) copy-start(bf16[8,512,2048]{2,1,0:T(8,128)(2,1)} %get-tuple-element.425) | copy-start | bytes 50331652
  555.3 107.1 %reduce-scatter.3.cloned.1.call-start = ((), (), s32[]{:S(2)}) async-start(), calls=%async_computation.3 | async-start | bytes 2228224 | tf_op jit(solution)/shard_map/reduce_scatter | solution.py:92
Sparse Core Ops, SparseCore 0:
  10.1 45.3 all-gather.7
  555.4 29.6 reduce-scatter.4
  588.9 73.3 reduce-scatter.2
where the time goes:
time: 673 us; the launch traced here: 669 us
  other arithmetic  325 us (48%)
  waiting for transfers between devices  129 us (19%)
  blocking collectives  120 us (18%)
  matrix products  32 us (5%)
  local copies, waits for them, and re-layouts  26.3 us (4%)
  loops' own time  21.8 us (3%)
  between operations  14.2 us (2%)
    all_gather x6, blocking collectives, combine(): parts = lax.all_gather(part, axis, axis=0)  107 us
    reduce_scatter x1, waiting for transfers between devices, local(): lax.psum_scatter(2.0 * (weight[:, None] * own - pulled), 'col', scatter_d...  77.2 us
    reduce_sum x24, other arithmetic, single(): return (peak, jnp.sum(jnp.exp(scores - peak[:, None]), axis=1))  74.8 us
    reduce_sum x24, other arithmetic, advance(): jnp.sum(jnp.exp(scores - new_peak[None, :]), axis=0)  74.4 us
    reduce_max x24, other arithmetic, single(): peak = jnp.max(scores, axis=1)  64.3 us
    reduce_max x24, other arithmetic, advance(): new_peak = jnp.maximum(peak, jnp.max(scores, axis=0))  64.1 us
    dynamic_update_slice x8, other arithmetic, local(): plan = lax.map(plan_rows, blocks).reshape(rows, cols)  34.6 us
    all_gather x1, waiting for transfers between devices, local(): imu_rows = lax.all_gather(imu, 'col', axis=0, tiled=True)  33.4 us
  transfers between devices with their start and end apart: 3, of which 3 were waited for; matrix products, arithmetic and copies ran while one was open for 2% of the time, Pallas kernels for 0%

commit v1 on v0

--- a/solution.py
+++ b/solution.py
@@ -6,6 +6,24 @@
 
 D = 128
 ITERS = 3
+
+
+def collect(array, axis, dim):
+    ways, here, step = (lax.axis_size(axis), lax.axis_index(axis), array.shape[dim])
+    shape = [n * ways if d == dim else n for d, n in enumerate(array.shape)]
+    full = lax.dynamic_update_slice_in_dim(
+        jnp.zeros(shape, array.dtype), array, here * step, axis=dim
+    )
+    going_up = going_down = array
+    for far in range(1, ways // 2 + 1):
+        going_up = lax.ppermute(going_up, axis, [(d, (d + 1) % ways) for d in range(ways)])
+        full = lax.dynamic_update_slice_in_dim(full, going_up, (here - far) % ways * step, axis=dim)
+        if 2 * far < ways:
+            going_down = lax.ppermute(going_down, axis, [(d, (d - 1) % ways) for d in range(ways)])
+            full = lax.dynamic_update_slice_in_dim(
+                full, going_down, (here + far) % ways * step, axis=dim
+            )
+    return full
 
 
 def cost_block(rows, rows_sq, cols, cols_sq):
@@ -26,7 +44,7 @@
 def local(imu, camera, imu_mass, cam_mass):
     epsilon = D / 20.0
     imu_rows = lax.all_gather(imu, "col", axis=0, tiled=True)
-    cam_rows = lax.all_gather(camera, "row", axis=1, tiled=True)[0]
+    cam_rows = collect(camera, "row", 1)[0]
     rows = imu_rows.shape[0]
     cols = cam_rows.shape[0]
     block = math.gcd(rows, 512)

time: 673 us -> 711 us (1.056)
  local copies, waits for them, and re-layouts: 26.3 us -> 62.4 us
  blocking collectives: 120 us -> 107 us
  starting transfers between devices: 0.12 us -> 8.93 us
    while x24 -> x25, local copies, waits for them, and re-layouts: 0.06 us -> 33.4 us  [the longest x1 33.3 us: row_lse(): peak, total = lax.map(single, blocks)]
    all_gather x1 -> x0, blocking collectives: 13.8 us -> none  [local(): cam_rows = lax.all_gather(camera, 'row', axis=1, tiled=True)[0]]
    ppermute x0 -> x7, waiting for transfers between devices: none -> 9.65 us  [the longest x4 9.58 us: collect(): lax.ppermute(going_up, axis, [(d, (d + 1) % ways) for d in range(ways)])]
    ppermute x0 -> x7, starting transfers between devices: none -> 8.82 us  [the longest x3 8.79 us: collect(): lax.ppermute(going_down, axis, [(d, (d - 1) % ways) for d in range(ways)])]
  transfers between devices with their start and end apart: 3 -> 10, of which waited for: 3 -> 8; matrix products, arithmetic and copies ran while one was open for 2% -> 2% of each run, Pallas kernels for 0% -> 0%
where the time goes in v1:
time: 711 us; the launch traced here: 706 us
  other arithmetic  325 us (46%)
  waiting for transfers between devices  133 us (19%)
  blocking collectives  107 us (15%)
  local copies, waits for them, and re-layouts  62.4 us (9%)
  matrix products  32 us (5%)
  loops' own time  24 us (3%)
  between operations  14.4 us (2%)
  starting transfers between devices  8.93 us (1%)
    all_gather x6, blocking collectives, combine(): parts = lax.all_gather(part, axis, axis=0)  107 us
    reduce_scatter x1, waiting for transfers between devices, local(): lax.psum_scatter(2.0 * (weight[:, None] * own - pulled), 'col', scatter_d...  77.2 us
    reduce_sum x24, other arithmetic, single(): return (peak, jnp.sum(jnp.exp(scores - peak[:, None]), axis=1))  74.8 us
    reduce_sum x24, other arithmetic, advance(): jnp.sum(jnp.exp(scores - new_peak[None, :]), axis=0)  74.4 us
    reduce_max x24, other arithmetic, single(): peak = jnp.max(scores, axis=1)  64.3 us
    reduce_max x24, other arithmetic, advance(): new_peak = jnp.maximum(peak, jnp.max(scores, axis=0))  64.1 us
    dynamic_update_slice x8, other arithmetic, local(): plan = lax.map(plan_rows, blocks).reshape(rows, cols)  34.7 us
    while x1, local copies, waits for them, and re-layouts, row_lse(): peak, total = lax.map(single, blocks)  33.3 us
  transfers between devices with their start and end apart: 10, of which 8 were waited for; matrix products, arithmetic and copies ran while one was open for 2% of the time, Pallas kernels for 0%

profile of v1, /device:TPU:0, one launch (start us, length us, event | category | flops | bytes accessed | tf_op | source)
XLA Modules:
  0.0 706.2 jit_solution(15811998476709621810)
XLA Ops:
  22.2 4.9 collective-permute-done.6
  27.4 28.1 %all-gather.8.cloned.1.call-done = bf16[4096,128]{1,0:T(8,128)(2,1)} async-done(((bf16[256,128]{1,0:T(8,128)(2,1)}), bf16[4096,128]{1,0:T(8,128)(2,1)}) %all-gather.8.cloned.1.call-update) | async-done | bytes 1048592 | tf_op jit(solution)/shard_map/all_gather | solution.py:46
  57.4 14.3 %bitcast_subtract_fusion = f32[4096,2048]{0,1:T(8,128)} fusion(f32[2048]{0:T(1024)S(1)} %fusion.13, f32[4096]{0:T(1024)S(1)} %fusion.12, bf16[2048,128]{1,0:T(8,128)(2,1)S(1)} %bitcast_dynamic-update-slice_fusion, bf16[4096,128]{1,0:T(8,128)(2,1)} %all-gather.8.cloned.1.call-done), kind=kOutput, calls=%fused_computation.32 | convolution fusion | flops 2172649472 | bytes 35151872 | tf_op jit(solution)/shard_map/dot_general | solution.py:30
  71.7 33.3 %copy.20 = f32[4096,2048]{1,0:T(8,128)} copy(f32[4096,2048]{0,1:T(8,128)} %bitcast_subtract_fusion) | data formatting | bytes 67108864 | tf_op jit(solution)/shard_map/while | solution.py:70
  105.0 58.2 %while.94 = (s32[]{:T(128)}, f32[8,512]{1,0:T(8,128)S(1)}, f32[8,512]{1,0:T(8,128)S(1)}, s32[8]{0:T(128)S(1)}, f32[4096,2048]{1,0:T(8,128)}, /*index=5*/s32[]{:T(128)}, s32[1]{0:T(128)}, s32[]{:T(128)}, s32[]{:T(128)}) while((s32[]{:T(128)}, f32[8,512]{1,0:T(8,128)S(1)}, f32[8,512]{1,0:T(8,128)S(1)}, s32[8]{0:T(128)S(1)}, ...), condition=%wide.region_5.6_spmd, body=%wide.region_2.5_spmd.sunk | while | flops 7339014 | bytes 8403111 | solution.py:70
  163.3 23.1 %all-gather.3 = f32[16,1,4096]{2,1,0:T(1,128)S(1)} all-gather(f32[1,1,4096]{2,1,0:T(1,128)S(1)} %reshape.132), channel_id=1, replica_groups=mesh['row'=8,'col'=16] {'col'}, dimensions={0}, use_global_device_ids=true | all-gather | bytes 278528 | tf_op jit(solution)/shard_map/all_gather | solution.py:39
  186.8 47.5 %while.98 = (s32[]{:T(128)}, f32[2048]{0:T(1024)S(1)}, f32[2048]{0:T(1024)S(1)}, f32[4096]{0:T(1024)S(1)}, f32[4096,2048]{1,0:T(8,128)}, /*index=5*/s32[]{:T(128)}, s32[]{:T(128)}, s32[]{:T(128)}, s32[]{:T(128)}) while((s32[]{:T(128)}, f32[2048]{0:T(1024)S(1)}, f32[2048]{0:T(1024)S(1)}, f32[4096]{0:T(1024)S(1)}, ...), condition=%wide.region_11.12_spmd.clone, body=%wide.region_8.11_spmd.clone.sunk | while | flops 7350279 | bytes 8503458 | solution.py:88
  234.3 13.0 %all-gather = f32[16384]{0:T(1024)S(1)} all-gather(f32[2048]{0:T(1024)S(1)} %log_add_fusion.5), channel_id=2, replica_groups=mesh['row'=8,'col'=16] {'row'}, dimensions={0}, use_global_device_ids=true | all-gather | bytes 73728 | tf_op jit(solution)/shard_map/all_gather | solution.py:39
  247.5 58.3 %while.95 = (s32[]{:T(128)}, f32[8,512]{1,0:T(8,128)S(1)}, f32[8,512]{1,0:T(8,128)S(1)}, f32[2048]{0:T(1024)S(1)}, s32[8]{0:T(128)S(1)}, /*index=5*/f32[4096,204...) while((s32[]{:T(128)}, f32[8,512]{1,0:T(8,128)S(1)}, f32[8,512]{1,0:T(8,128)S(1)}, ...), condition=%wide.region_17.18_spmd, body=%wide.region_14.17_spmd.sunk | while | flops 7339014 | bytes 8419503 | solution.py:70
  305.8 21.7 %all-gather.4 = f32[16,1,4096]{2,1,0:T(1,128)S(1)} all-gather(f32[1,1,4096]{2,1,0:T(1,128)S(1)} %reshape.134), channel_id=1, replica_groups=mesh['row'=8,'col'=16] {'col'}, dimensions={0}, use_global_device_ids=true | all-gather | bytes 278528 | tf_op jit(solution)/shard_map/all_gather | solution.py:39
  327.9 47.5 %while.99 = (s32[]{:T(128)}, f32[2048]{0:T(1024)S(1)}, f32[2048]{0:T(1024)S(1)}, f32[4096]{0:T(1024)S(1)}, f32[4096,2048]{1,0:T(8,128)}, /*index=5*/s32[]{:T(128)}, s32[]{:T(128)}, s32[]{:T(128)}, s32[]{:T(128)}) while((s32[]{:T(128)}, f32[2048]{0:T(1024)S(1)}, f32[2048]{0:T(1024)S(1)}, f32[4096]{0:T(1024)S(1)}, ...), condition=%wide.region_23.24_spmd.clone, body=%wide.region_20.23_spmd.clone.sunk | while | flops 7350279 | bytes 8503458 | solution.py:88
  375.4 12.8 %all-gather.1 = f32[16384]{0:T(1024)S(1)} all-gather(f32[2048]{0:T(1024)S(1)} %log_add_fusion.4), channel_id=3, replica_groups=mesh['row'=8,'col'=16] {'row'}, dimensions={0}, use_global_device_ids=true | all-gather | bytes 73728 | tf_op jit(solution)/shard_map/all_gather | solution.py:39
  388.3 58.2 %while.96 = (s32[]{:T(128)}, f32[8,512]{1,0:T(8,128)S(1)}, f32[8,512]{1,0:T(8,128)S(1)}, f32[2048]{0:T(1024)S(1)}, s32[8]{0:T(128)S(1)}, /*index=5*/f32[4096,204...) while((s32[]{:T(128)}, f32[8,512]{1,0:T(8,128)S(1)}, f32[8,512]{1,0:T(8,128)S(1)}, ...), condition=%wide.region_29.30_spmd, body=%wide.region_26.29_spmd.sunk | while | flops 7339014 | bytes 8419503 | solution.py:70
  446.6 23.1 %all-gather.5 = f32[16,1,4096]{2,1,0:T(1,128)S(1)} all-gather(f32[1,1,4096]{2,1,0:T(1,128)S(1)} %reshape.136), channel_id=1, replica_groups=mesh['row'=8,'col'=16] {'col'}, dimensions={0}, use_global_device_ids=true | all-gather | bytes 278528 | tf_op jit(solution)/shard_map/all_gather | solution.py:39
  470.1 47.5 %while.100 = (s32[]{:T(128)}, f32[2048]{0:T(1024)S(1)}, f32[2048]{0:T(1024)S(1)}, f32[4096]{0:T(1024)S(1)}, f32[4096,2048]{1,0:T(8,128)}, /*index=5*/s32[]{:T(128)}, s32[]{:T(128)}, s32[]{:T(128)}, s32[]{:T(128)}) while((s32[]{:T(128)}, f32[2048]{0:T(1024)S(1)}, f32[2048]{0:T(1024)S(1)}, f32[4096]{0:T(1024)S(1)}, ...), condition=%wide.region_35.36_spmd.clone, body=%wide.region_32.35_spmd.clone.sunk | while | flops 7350279 | bytes 8503458 | solution.py:88
  517.6 13.0 %all-gather.2 = f32[16384]{0:T(1024)S(1)} all-gather(f32[2048]{0:T(1024)S(1)} %log_add_fusion.3), channel_id=4, replica_groups=mesh['row'=8,'col'=16] {'row'}, dimensions={0}, use_global_device_ids=true | all-gather | bytes 73728 | tf_op jit(solution)/shard_map/all_gather | solution.py:39
  530.7 45.3 %while.97 = (s32[]{:T(128)}, bf16[8,512,2048]{2,1,0:T(8,128)(2,1)}, s32[8]{0:T(128)S(1)}, f32[4096]{0:T(1024)S(1)}, f32[2048]{0:T(1024)S(1)}, /*index=5*/f32[409...) while((s32[]{:T(128)}, bf16[8,512,2048]{2,1,0:T(8,128)(2,1)}, s32[8]{0:T(128)S(1)}, ...), condition=%wide.region_39.40_spmd, body=%wide.region_38.39_spmd.sunk | while | flops 4194310 | bytes 6306471 | solution.py:101
  554.6 4.4 fusion.41
  566.0 4.4 fusion.41
  576.0 8.5 %convert_reduce_fusion = (f32[2048]{0:T(1024)S(1)}, f32[8,512]{1,0:T(8,128)S(1)}) fusion(bf16[8,512,2048]{2,1,0:T(8,128)(2,1)} %get-tuple-element.425), kind=kLoop, calls=%fused_computation.30 | loop fusion | flops 25159680 | bytes 16801792 | tf_op jit(solution)/shard_map/reduce_sum | solution.py:103
  586.7 6.0 fusion.15
  592.8 11.7 %fusion.11 = f32[4096,128]{1,0:T(8,128)} fusion(bf16[4096,2048]{1,0:T(8,128)(2,1)} %bitcast.82, bf16[2048,128]{1,0:T(8,128)(2,1)S(1)} %bitcast_dynamic-update-slice_fusion, bf16[4096,128]{1,0:T(8,128)(2,1)S(1)} %copy-done.1, f32[4096]{0:T(1024)S(1)} %bitcast.91), kind=kOutput, calls=%fused_computation.34 | convolution fusion | flops 2149580800 | bytes 20463616 | tf_op jit(solution)/shard_map/dot_general | solution.py:109
  604.5 18.1 %reduce-scatter.5.cloned.1.call-done = f32[256,128]{1,0:T(8,128)} async-done(((f32[2048,128]{1,0:T(8,128)}), f32[256,128]{1,0:T(8,128)}) %reduce-scatter.5.cloned.1.call-update) | async-done | bytes 131088 | tf_op jit(solution)/shard_map/reduce_scatter | solution.py:119
  622.6 77.2 %reduce-scatter.3.cloned.1.call-done = f32[256,128]{1,0:T(8,128)} async-done(((f32[4096,128]{1,0:T(8,128)}), f32[256,128]{1,0:T(8,128)}) %reduce-scatter.3.cloned.1.call-update) | async-done | bytes 131088 | tf_op jit(solution)/shard_map/reduce_scatter | solution.py:110
  (372 shorter events, 350.5 us)
Async XLA Ops:
  7.2 48.4 %all-gather.8.cloned.1.call-start = ((), (), s32[]{:S(2)}) async-start(), calls=%async_computation.2 | async-start | bytes 1114112 | tf_op jit(solution)/shard_map/all_gather | solution.py:46
  7.2 5.1 collective-permute-start
  7.2 5.2 collective-permute-start.1
  10.2 612.4 %reduce-scatter.5.cloned.1.call-start = ((), (), s32[]{:S(2)}) async-start(), calls=%async_computation.4 | async-start | bytes 1179648 | tf_op jit(solution)/shard_map/reduce_scatter | solution.py:119
  12.3 4.9 collective-permute-start.2
  12.4 4.8 collective-permute-start.3
  17.2 4.9 collective-permute-start.4
  17.2 4.9 collective-permute-start.5
  22.1 4.9 collective-permute-start.6
  105.0 81.7 %copy-start.2 = (f32[4096]{0:T(1024)S(1)}, f32[4096]{0:T(1024)}, u32[]{:S(2)}) copy-start(f32[4096]{0:T(1024)} %param.20) | copy-start | bytes 49156
  186.8 60.7 %copy-start.3 = (f32[2048]{0:T(1024)S(1)}, f32[2048]{0:T(1024)}, u32[]{:S(2)}) copy-start(f32[2048]{0:T(1024)} %param.21) | copy-start | bytes 24580
  530.7 53.8 %copy-start.1 = (bf16[4096,128]{1,0:T(8,128)(2,1)S(1)}, bf16[4096,128]{1,0:T(8,128)(2,1)}, u32[]{:S(2)}) copy-start(bf16[4096,128]{1,0:T(8,128)(2,1)} %all-gather.8.cloned.1.call-done) | copy-start | bytes 3145732
  576.0 10.7 %copy-start = (bf16[8,512,2048]{2,1,0:T(8,128)(2,1)S(1)}, bf16[8,512,2048]{2,1,0:T(8,128)(2,1)}, u32[]{:S(2)}) copy-start(bf16[8,512,2048]{2,1,0:T(8,128)(2,1)} %get-tuple-element.425) | copy-start | bytes 50331652
  592.7 107.0 %reduce-scatter.3.cloned.1.call-start = ((), (), s32[]{:S(2)}) async-start(), calls=%async_computation.3 | async-start | bytes 2228224 | tf_op jit(solution)/shard_map/reduce_scatter | solution.py:110
Sparse Core Ops, SparseCore 0:
  10.3 45.1 all-gather.7
  592.9 29.6 reduce-scatter.4
  626.4 73.2 reduce-scatter.2
